TPU v7x, 32 devices: a whole 2x2x4 slice. The times are simulated.
32 devices in a mesh: shot: 2 (over x), strip: 16 (over z, y, core).
Axes of the slice: x: 2, y: 2, z: 4, core: 2. Of those that a mesh axis runs over, the one named last changes fastest.
Arguments:
- waves: float32 [2, 2, 8, 512, 512], P(None, None, 'shot', 'strip'), parts along dimension 2, may hold values from -6 to 6
- levels: int32 [512, 512], P('strip'), may hold values from 0 to 4
- coeffs: float32 [2, 4, 5, 17], replicated, may hold values from -0.7 to 0.7
- angles: float32 [4, 5], replicated, may hold values from -3.140625 to 3.140625
- order: int32 [8], P('shot'), parts along dimension 0, may hold values from 0 to 3, each once
Outputs:
- waves_out: float32 [2, 2, 8, 512, 512], P(None, None, 'shot', 'strip'), parts along dimension 2
- image: float32 [4, 512, 512], P('shot', 'strip'), parts along dimension 0
There are 2 independent parts, one for each index of `shot`. A program takes and returns all parts, laid end to end along the dimension named above; an argument that names none is the same for every part. Nothing has to cross between parts.
Inputs may be any that keep to these rules, and one draw needn't show every extreme that they name: order names every table row once.
All inputs are finite; a program needn't handle non-finite values.
Results may differ from a plain program's by a relative error of at most 0.00013.
Values sent between devices are 32-bit elements; how exact they have to be, the bound alone decides.
A program may use at most 64 MiB of HBM per device.

v0:
```python
import functools

import jax
import jax.numpy as jnp
from jax import lax
from jax.experimental import pallas as pl
from jax.experimental.pallas import tpu as pltpu
from jax.sharding import PartitionSpec as P

STEPS = 2
LANES = 128
SUBS = 8
ROWS = 4
PAIR = 2
MESH = pl.DeviceIdType.MESH


def tile_rows(index, count=1):
    return pl.ds(pl.multiple_of(index * SUBS, SUBS), count * SUBS)


def kernel(
    sizes, waves_hbm, levels_hbm, coeffs_hbm, angles_ref, order_ref, out_ref, image_ref,
    waves_ref, levels_ref, coeffs_ref, load_sem,
    level_buf, table_buf, coef_buf, turn_buf, field_buf, mid_buf, image_buf, send_sem, recv_sem,
):
    freqs, rows, blocks, per_tile, groups, levels, taps, strips = sizes
    half = taps // 2
    span = rows + 2 * half
    me = lax.axis_index("strip")
    has_low, has_high = me > 0, me < strips - 1

    loads = [
        pltpu.make_async_copy(source, target, load_sem.at[i])
        for i, (source, target) in enumerate(
            ((coeffs_hbm, coeffs_ref), (levels_hbm, levels_ref), (waves_hbm, waves_ref))
        )
    ]
    for load in loads:
        load.start()

    def neighbour(step):
        return {"strip": me + step}

    barrier = pltpu.get_barrier_semaphore()
    for there, step in ((has_low, -1), (has_high, 1)):

        @pl.when(there)
        def _():
            pl.semaphore_signal(barrier, inc=1, device_id=neighbour(step), device_id_type=MESH)

    lane = lax.broadcasted_iota(jnp.int32, (SUBS, LANES), 1)
    sub = lax.broadcasted_iota(jnp.int32, (SUBS, LANES), 0)
    block_of = lax.rem(sub, blocks)

    loads[1].wait()
    for top in range(0, rows, SUBS):
        for block in range(blocks):
            cells = levels_ref[top : top + SUBS, block * LANES : (block + 1) * LANES]
            for member in range(per_tile):
                level_buf[pl.ds(top * SUBS + member * blocks + block, SUBS, stride=SUBS), :] = cells

    def table_at(group, tap, part, level):
        return tile_rows(((group * taps + tap) * 2 + part) * levels + level)

    def by_member(values):
        tile = jnp.full((SUBS, LANES), values[0], jnp.float32)
        for member in range(1, per_tile):
            tile = jnp.where(sub >= member * blocks, values[member], tile)
        return tile

    loads[0].wait()
    slots = [order_ref[f] for f in range(freqs)]
    turn_tabs = []
    for group in range(groups):
        members = slots[group * per_tile : (group + 1) * per_tile]
        turn = jnp.zeros((SUBS, LANES), jnp.float32)
        for level in range(levels):
            for tap in range(taps):
                for part in range(2):
                    table_buf[table_at(group, tap, part, level), :] = by_member(
                        [coeffs_ref[part, row, level, tap] for row in members]
                    )
            turn = jnp.where(lane == level, by_member([angles_ref[row, level] for row in members]), turn)
        for which, tab in enumerate((jnp.cos(turn), jnp.sin(turn))):
            turn_tabs.append([jnp.broadcast_to(tab[:, level : level + 1], (SUBS, LANES)) for level in range(levels)])

    def coef_at(group, y, tap, part):
        return tile_rows(((group * rows + y) * taps + tap) * 2 + part)

    def turn_at(group, y, which):
        return tile_rows((group * rows + y) * 2 + which)

    def choose(masks, entries):
        tile = entries[0]
        for mask, entry in zip(masks, entries[1:]):
            tile = jnp.where(mask, entry, tile)
        return tile

    @pl.loop(0, rows // PAIR)
    def _(trip):
        y = trip * PAIR
        masks = []
        for place in range(PAIR):
            level_tile = level_buf[tile_rows(y + place), :]
            masks.append([level_tile == level for level in range(1, levels)])
        for group in range(groups):
            for which in range(2):
                for place in range(PAIR):
                    turn_buf[turn_at(group, y + place, which), :] = choose(masks[place], turn_tabs[group * 2 + which])
            for tap in range(taps):
                for part in range(2):
                    entries = [table_buf[table_at(group, tap, part, level), :] for level in range(levels)]
                    for place in range(PAIR):
                        coef_buf[coef_at(group, y + place, tap, part), :] = choose(masks[place], entries)

    def field_at(group, comp, y):
        return tile_rows((group * 4 + comp) * rows + y)

    def mid_at(step, group, y, comp):
        return tile_rows(((step * groups + group) * span + y) * 4 + comp)

    loads[2].wait()
    for group in range(groups):
        for comp in range(4):
            for member in range(per_tile):
                for top in range(0, rows, SUBS):
                    for block in range(blocks):
                        cells = waves_ref[
                            comp // 2, comp % 2, group * per_tile + member, top : top + SUBS,
                            block * LANES : (block + 1) * LANES,
                        ]
                        start = ((group * 4 + comp) * rows + top) * SUBS + member * blocks + block
                        field_buf[pl.ds(start, SUBS, stride=SUBS), :] = cells

    for there, first in ((has_low, 0), (has_high, rows + half)):

        @pl.when(jnp.logical_not(there))
        def _():
            for step in range(STEPS):
                for group in range(groups):

                    @pl.loop(0, half * 4)
                    def _(i):
                        mid_buf[tile_rows(((step * groups + group) * span + first) * 4 + i), :] = jnp.zeros(
                            (SUBS, LANES), jnp.float32
                        )

    pl.semaphore_wait(barrier, has_low.astype(jnp.int32) + has_high.astype(jnp.int32))

    def halo_copy(step, group, side):
        source, target = ((half, rows + half), (rows, 0))[side]
        base = (step * groups + group) * span
        return pltpu.make_async_remote_copy(
            src_ref=mid_buf.at[tile_rows((base + source) * 4, half * 4)],
            dst_ref=mid_buf.at[tile_rows((base + target) * 4, half * 4)],
            send_sem=send_sem.at[step, group, side],
            recv_sem=recv_sem.at[step, group, side],
            device_id=neighbour((-1, 1)[side]),
            device_id_type=MESH,
        )

    def inline_row(step, group, y):
        cosine = turn_buf[turn_at(group, y, 0), :]
        sine = turn_buf[turn_at(group, y, 1), :]
        sr, si, rr, ri = [field_buf[field_at(group, comp, y), :] for comp in range(4)]
        cells = (sr * cosine - si * sine, sr * sine + si * cosine, rr * cosine + ri * sine, ri * cosine - rr * sine)
        before = [jnp.where(block_of == 0, 0.0, pltpu.roll(v, 1, 0)) for v in cells]
        after = [jnp.where(block_of == blocks - 1, 0.0, pltpu.roll(v, SUBS - 1, 0)) for v in cells]
        acc = [None] * 4
        for tap in range(taps):
            shift = tap - half
            if shift < 0:
                moved = [
                    pltpu.roll(jnp.where(lane < LANES + shift, v, w), -shift, 1) for v, w in zip(cells, before)
                ]
            elif shift > 0:
                moved = [
                    pltpu.roll(jnp.where(lane >= shift, v, w), LANES - shift, 1) for v, w in zip(cells, after)
                ]
            else:
                moved = cells
            add_tap(acc, group, y, tap, moved)
        for comp in range(4):
            mid_buf[mid_at(step, group, y + half, comp), :] = acc[comp]

    def add_tap(acc, group, y, tap, moved):
        cr = coef_buf[coef_at(group, y, tap, 0), :]
        ci = coef_buf[coef_at(group, y, tap, 1), :]
        sr, si, rr, ri = moved
        if acc[0] is None:
            acc[:] = [cr * sr - ci * si, cr * si + ci * sr, cr * rr + ci * ri, cr * ri - ci * rr]
        else:
            acc[0] = acc[0] + cr * sr - ci * si
            acc[1] = acc[1] + cr * si + ci * sr
            acc[2] = acc[2] + cr * rr + ci * ri
            acc[3] = acc[3] + cr * ri - ci * rr

    def trips(first, last, inline=None, cross=None):
        @pl.loop(first // ROWS, last // ROWS)
        def _(trip):
            for place in range(ROWS):
                if inline is not None:
                    inline_row(*inline, trip * ROWS + place)
                if cross is not None and place % PAIR == 0:
                    cross_rows(*cross, trip * ROWS + place)

    def send(step, group):
        for side, there in enumerate((has_low, has_high)):

            @pl.when(there)
            def _():
                halo_copy(step, group, side).start()

    def receive(step, group):
        for side, there in ((1, has_low), (0, has_high)):

            @pl.when(there)
            def _():
                halo_copy(step, group, side).wait_recv()

    def cross_rows(step, group, y):
        accs = [[None] * 4 for _ in range(PAIR)]
        for line in range(taps + PAIR - 1):
            moved = [mid_buf[mid_at(step, group, y + line, comp), :] for comp in range(4)]
            for place in range(PAIR):
                if 0 <= line - place < taps:
                    add_tap(accs[place], group, y + place, line - place, moved)
        for place, acc in enumerate(accs):
            for comp in range(4):
                field_buf[field_at(group, comp, y + place), :] = acc[comp]
            term = acc[0] * acc[2] + acc[1] * acc[3]
            at = tile_rows(step * rows + y + place)
            if group == 0:
                image_buf[at, :] = term
            else:
                image_buf[at, :] = image_buf[at, :] + term

    passes = [(step, group) for step in range(STEPS) for group in range(groups)]
    pending = []
    for step, group in passes:
        here = (step, group)
        beside = None
        if group == 0 and pending:
            while len(pending) > 1 or pending[0][1] == 0:
                before = pending.pop(0)
                receive(*before)
                trips(0, rows, cross=before)
            before = pending.pop(0)
            receive(*before)
            trips(0, half, here, before)
            trips(rows - half, rows, here, before)
            send(*here)
            trips(half, rows - half, here, before)
        else:
            trips(0, half, here)
            trips(rows - half, rows, here)
            send(*here)
            if pending:
                before = pending.pop(0)
                receive(*before)
                trips(half, rows - half, here, before)
                trips(0, half, cross=before)
                trips(rows - half, rows, cross=before)
            else:
                trips(half, rows - half, here)
        pending.append(here)
    for before in pending:
        receive(*before)
        trips(0, rows, cross=before)

    for group in range(groups):
        for comp in range(4):
            for member in range(per_tile):
                for top in range(0, rows, SUBS):
                    for block in range(blocks):
                        start = ((group * 4 + comp) * rows + top) * SUBS + member * blocks + block
                        out_ref[
                            comp // 2, comp % 2, group * per_tile + member, top : top + SUBS,
                            block * LANES : (block + 1) * LANES,
                        ] = field_buf[pl.ds(start, SUBS, stride=SUBS), :]
    for step in range(STEPS):
        for top in range(0, rows, SUBS):
            for block in range(blocks):
                total = None
                for member in range(per_tile):
                    start = (step * rows + top) * SUBS + member * blocks + block
                    term = image_buf[pl.ds(start, SUBS, stride=SUBS), :]
                    total = term if total is None else total + term
                image_ref[step, top : top + SUBS, block * LANES : (block + 1) * LANES] = total

    for step in range(STEPS):
        for group in range(groups):
            for side, there in enumerate((has_low, has_high)):

                @pl.when(there)
                def _():
                    halo_copy(step, group, side).wait_send()


def on_device(strips, waves, levels, coeffs, angles, order):
    freqs, rows, cells = waves.shape[2:]
    level_count, taps = coeffs.shape[2:]
    blocks = cells // LANES
    per_tile = SUBS // blocks
    groups = freqs // per_tile
    assert blocks * per_tile == SUBS and groups * per_tile == freqs
    assert rows % SUBS == 0 and rows >= taps - 1 and level_count * taps <= LANES
    half = taps // 2
    sizes = (freqs, rows, blocks, per_tile, groups, level_count, taps, strips)
    tiles = lambda count: pltpu.VMEM((count * SUBS, LANES), jnp.float32)
    vmem, smem, hbm = [pl.BlockSpec(memory_space=space) for space in (pltpu.VMEM, pltpu.SMEM, pltpu.HBM)]
    return pl.pallas_call(
        functools.partial(kernel, sizes),
        out_shape=(
            jax.ShapeDtypeStruct(waves.shape, jnp.float32),
            jax.ShapeDtypeStruct((STEPS, rows, cells), jnp.float32),
        ),
        in_specs=[hbm, hbm, hbm, smem, smem],
        out_specs=(vmem, vmem),
        scratch_shapes=[
            pltpu.VMEM(waves.shape, jnp.float32),
            pltpu.VMEM(levels.shape, jnp.int32),
            pltpu.SMEM(coeffs.shape, jnp.float32),
            pltpu.SemaphoreType.DMA((3,)),
            pltpu.VMEM((rows * SUBS, LANES), jnp.int32),
            tiles(groups * taps * 2 * level_count),
            tiles(groups * rows * taps * 2),
            tiles(groups * rows * 2),
            tiles(groups * 4 * rows),
            tiles(STEPS * groups * (rows + 2 * half) * 4),
            tiles(STEPS * rows),
            pltpu.SemaphoreType.DMA((STEPS, groups, 2)),
            pltpu.SemaphoreType.DMA((STEPS, groups, 2)),
        ],
        compiler_params=pltpu.CompilerParams(
            collective_id=0, has_side_effects=True, vmem_limit_bytes=67043328 - 1250000
        ),
    )(waves, levels, coeffs, angles, order)


def solution(mesh):
    in_specs = (P(None, None, "shot", "strip", None), P("strip", None), P(), P(), P("shot"))
    out_specs = (P(None, None, "shot", "strip", None), P("shot", "strip", None))
    return jax.shard_map(
        functools.partial(on_device, mesh.shape["strip"]),
        mesh=mesh,
        in_specs=in_specs,
        out_specs=out_specs,
        check_vma=False,
    )
```

profile of v0, /device:TPU:12, one launch (start us, length us, event | category | flops | bytes accessed | tf_op | source)
XLA Modules:
  0.0 30.2 jit_solution(6700932127013702524)
XLA Ops:
  0.6 1.4 %copy.7.coeffs_hbm = f32[2,4,5,17]{3,2,1,0:T(8,128)} copy(f32[2,4,5,17]{3,1,2,0:T(4,128)} %param.7) | data formatting | bytes 5440 | tf_op args[2]
  2.0 25.2 %shard_map.68 = (f32[2,2,4,32,512]{4,3,2,1,0:T(8,128)}, f32[2,32,512]{2,1,0:T(8,128)}) custom-call(f32[2,2,4,32,512]{4,3,2,1,0:T(8,128)} %waves_hbm.1, s32[32,512]{1,0:T(8,128)} %levels_hbm.1, f32[2,4,5,17]{3,2,1,0:T(8,128)} %copy.7.coeffs_hbm, f32[4,5]{1,0:T(4,128)} %angles_ref.1, s32[4]{0:T(128)} %order_ref.1), custom_call_target="tpu_custom_call" | custom-call | tf_op jit(solution)/shard_map/pallas_call | solution.py:313
  27.2 0.0 copy-start
  27.2 2.3 %copy.10 = f32[2,2,4,32,512]{4,3,2,1,0:T(8,128)} copy(f32[2,2,4,32,512]{4,3,2,1,0:T(8,128)} %get-tuple-element.4) | data formatting | bytes 2097152
  29.5 0.0 copy-done
  29.6 0.7 %copy.11 = f32[2,32,512]{2,1,0:T(8,128)} copy(f32[2,32,512]{2,1,0:T(8,128)S(1)} %copy-done) | data formatting | bytes 262144
Async XLA Ops:
  27.2 2.3 %copy-start = (f32[2,32,512]{2,1,0:T(8,128)S(1)}, f32[2,32,512]{2,1,0:T(8,128)}, u32[]{:S(2)}) copy-start(f32[2,32,512]{2,1,0:T(8,128)} %get-tuple-element.5) | copy-start | bytes 393220
where the time goes:
time: 30.4 us; the launch traced here: 30.2 us
  Pallas kernels  25.2 us (83%)
  local copies, waits for them, and re-layouts  4.33 us (14%)
  between operations  0.65 us (2%)
    pallas_call x1, Pallas kernels, on_device(): pl.pallas_call(functools.partial(kernel, sizes), out_shape=(jax.ShapeDtyp...  25.2 us
    unnamed x5, local copies, waits for them, and re-layouts  4.33 us

commit v1 on v0

v1 whole, which is shorter than its diff:
```python
import functools

import jax
import jax.numpy as jnp
from jax import lax
from jax.experimental import pallas as pl
from jax.experimental.pallas import tpu as pltpu
from jax.sharding import PartitionSpec as P

STEPS = 2
LANES = 128
SUBS = 8
WIN = 16
MESH = pl.DeviceIdType.MESH


def split(v):
    high = v.astype(jnp.bfloat16)
    low = (v - high.astype(jnp.float32)).astype(jnp.bfloat16)
    return high, low


def pick(level, entries):
    out = entries[0]
    for i, entry in enumerate(entries[1:], 1):
        out = jnp.where(level == i, entry, out)
    return out


def filtered(table, parts, level):
    (hr, hi), (lr, li) = parts
    sums = jnp.dot(
        table, jnp.concatenate([hr, hi, lr, li, hr, hi], axis=0), preferred_element_type=jnp.float32
    )
    count = sums.shape[0] // (2 * WIN)
    return [
        pick(level, [sums[(2 * i + comp) * WIN : (2 * i + comp + 1) * WIN] for i in range(count)])
        for comp in range(2)
    ]


def kernel(
    sizes, waves_hbm, levels_hbm, coeffs_hbm, angles_hbm, order_hbm, out_ref, image_ref,
    order_ref, level_ref, coef_ref, angle_ref, load_sem,
    turned_ref, base_ref, turn_ref, table_ref, cos_ref, sin_ref,
    field_ref, part_ref, pass_ref, mid_ref, cross_ref, send_sem, recv_sem,
):
    freqs, rows, cells, levels, taps, strips = sizes
    half = taps // 2
    blocks = cells // LANES
    me = lax.axis_index("strip")
    has_low, has_high = me > 0, me < strips - 1

    small = [
        pltpu.make_async_copy(source, target, load_sem.at[i])
        for i, (source, target) in enumerate(
            ((coeffs_hbm, coef_ref), (angles_hbm, angle_ref), (levels_hbm, level_ref), (order_hbm, order_ref))
        )
    ]
    for load in small:
        load.start()

    def wave_load(f):
        return pltpu.make_async_copy(waves_hbm.at[:, :, f], field_ref.at[f], load_sem.at[4 + f])

    for f in range(freqs):
        wave_load(f).start()

    def neighbour(step):
        return {"strip": me + step}

    barrier = pltpu.get_barrier_semaphore()
    for there, step in ((has_low, -1), (has_high, 1)):

        @pl.when(there)
        def _():
            pl.semaphore_signal(barrier, inc=1, device_id=neighbour(step), device_id_type=MESH)

    lane = lax.broadcasted_iota(jnp.int32, (SUBS, LANES), 1)

    for there, first in ((has_low, 0), (has_high, rows + half)):

        @pl.when(jnp.logical_not(there))
        def _():
            for step in range(STEPS):

                @pl.loop(0, freqs)
                def _(f):
                    for field in range(2):
                        for comp in range(2):
                            mid_ref[step, f, field, comp, first : first + half, :] = jnp.zeros(
                                (half, cells), jnp.float32
                            )

    base_ref[...] = jnp.zeros_like(base_ref)
    small[0].wait()
    for comp in range(2):
        for level in range(levels):
            base_ref[comp, level, :, :taps] = coef_ref[comp, level]
    for level in range(levels):
        real, imag = base_ref[0, level], base_ref[1, level]
        for comp, (first, second) in enumerate(((real, -imag), (imag, real))):
            both = first + pltpu.roll(second, 2 * WIN, 1)
            base_ref[comp, level] = both + pltpu.roll(both, 4 * WIN, 1)

    small[1].wait()
    turn_ref[...] = jnp.zeros_like(turn_ref)
    angle = angle_ref[...]
    turn_ref[0, :, :levels] = jnp.cos(angle)
    turn_ref[1, :, :levels] = jnp.sin(angle)

    small[2].wait()
    small[3].wait()
    stacked = jnp.concatenate([level_ref[:, q * LANES : (q + 1) * LANES] for q in range(blocks)], axis=0)
    turned_ref[...] = stacked.T

    def prepare(f):
        row = pl.ds(order_ref[f], 1)
        for level in range(levels):
            for comp in range(2):
                line = jnp.broadcast_to(base_ref[comp, level, row, :], (WIN, LANES))
                high, low = split(pltpu.roll(line, 0, 1, stride=1, stride_axis=0))
                at = (2 * level + comp) * WIN
                table_ref[f, at : at + WIN, :LANES] = high
                table_ref[f, at : at + WIN, LANES:] = low[:, : 4 * WIN]
        for which, target in enumerate((cos_ref, sin_ref)):
            line = turn_ref[which, row, :]
            entries = [jnp.broadcast_to(line[:, i : i + 1], (SUBS, LANES)) for i in range(levels)]
            for top in range(0, rows, SUBS):
                for q in range(blocks):
                    level = level_ref[top : top + SUBS, q * LANES : (q + 1) * LANES]
                    target[f, top : top + SUBS, q * LANES : (q + 1) * LANES] = pick(level, entries)

    def inline_pass(step, f):
        cosine, sine = cos_ref[f], sin_ref[f]
        for field in range(2):
            real, imag = field_ref[f, field, 0], field_ref[f, field, 1]
            if step == 0 and field == 1:
                imag = -imag
            turned = (real * cosine - imag * sine, real * sine + imag * cosine)
            for comp in range(2):
                v = turned[comp]
                v = jnp.concatenate([v[:, q * LANES : (q + 1) * LANES] for q in range(blocks)], axis=0).T
                before = jnp.where(lane >= rows, pltpu.roll(v[LANES - half :], rows, 1), 0.0)
                after = jnp.where(lane < LANES - rows, pltpu.roll(v[:half], LANES - rows, 1), 0.0)
                for part, piece in enumerate(split(jnp.concatenate([before, v, after], axis=0))):
                    part_ref[part, comp, :, field * LANES : (field + 1) * LANES] = piece
        table = table_ref[f]
        for b in range(0, LANES, WIN):
            parts = [[part_ref[part, comp, b : b + 2 * WIN, :] for comp in range(2)] for part in range(2)]
            level = turned_ref[b : b + WIN, :]
            sums = filtered(table, parts, jnp.concatenate([level, level], axis=1))
            for comp in range(2):
                pass_ref[comp, b : b + WIN, :] = sums[comp]
        for field in range(2):
            for comp in range(2):
                v = pass_ref[comp, :, field * LANES : (field + 1) * LANES].T
                for q in range(blocks):
                    mid_ref[step, f, field, comp, half : half + rows, q * LANES : (q + 1) * LANES] = v[
                        q * rows : (q + 1) * rows
                    ]

    def cross_pass(step, f):
        last = step == STEPS - 1
        for field in range(2):
            for comp in range(2):
                for part, piece in enumerate(split(mid_ref[step, f, field, comp])):
                    cross_ref[part, field, comp] = piece
        table = table_ref[f]
        wide = 2 * LANES
        for b in range(0, rows, WIN):
            for x in range(0, cells, wide):
                at = (slice(b, b + WIN), slice(x, x + wide))
                level = level_ref[at]
                sums = []
                for field in range(2):
                    parts = [
                        [cross_ref[part, field, comp, b : b + 2 * WIN, x : x + wide] for comp in range(2)]
                        for part in range(2)
                    ]
                    sums.append(filtered(table, parts, level))
                (sr, si), (qr, qi) = sums
                for field in range(2):
                    for comp in range(2):
                        v = sums[field][comp]
                        if last:
                            out_ref[(field, comp, f) + at] = -v if field and comp else v
                        else:
                            field_ref[(f, field, comp) + at] = v
                image_ref[(step,) + at] += sr * qr - si * qi

    def halo_copy(step, f, side):
        source, target = ((half, rows + half), (rows, 0))[side]
        return pltpu.make_async_remote_copy(
            src_ref=mid_ref.at[step, f, :, :, pl.ds(source, half), :],
            dst_ref=mid_ref.at[step, f, :, :, pl.ds(target, half), :],
            send_sem=send_sem.at[step, f, side],
            recv_sem=recv_sem.at[step, f, side],
            device_id=neighbour((-1, 1)[side]),
            device_id_type=MESH,
        )

    def send(step, f):
        for side, there in enumerate((has_low, has_high)):

            @pl.when(there)
            def _():
                halo_copy(step, f, side).start()

    def receive(step, f):
        for side, there in ((1, has_low), (0, has_high)):

            @pl.when(there)
            def _():
                halo_copy(step, f, side).wait_recv()

    image_ref[...] = jnp.zeros_like(image_ref)

    prepare(0)
    wave_load(0).wait()
    inline_pass(0, 0)
    pl.semaphore_wait(barrier, has_low.astype(jnp.int32) + has_high.astype(jnp.int32))
    send(0, 0)

    @pl.loop(1, freqs)
    def _(f):
        prepare(f)
        wave_load(f).wait()
        inline_pass(0, f)
        send(0, f)

    @pl.loop(0, freqs)
    def _(f):
        receive(0, f)
        cross_pass(0, f)
        inline_pass(1, f)
        send(1, f)

    @pl.loop(0, freqs)
    def _(f):
        receive(1, f)
        cross_pass(1, f)

    for step in range(STEPS):

        @pl.loop(0, freqs)
        def _(f):
            for side, there in enumerate((has_low, has_high)):

                @pl.when(there)
                def _():
                    halo_copy(step, f, side).wait_send()


def store_kernel(waves_ref, image_ref, waves_hbm, image_hbm, sem):
    copies = [
        pltpu.make_async_copy(waves_ref, waves_hbm, sem.at[0]),
        pltpu.make_async_copy(image_ref, image_hbm, sem.at[1]),
    ]
    for copy in copies:
        copy.start()
    for copy in copies:
        copy.wait()


def on_device(strips, waves, levels, coeffs, angles, order):
    freqs, rows, cells = waves.shape[2:]
    level_count, taps = coeffs.shape[2:]
    half = taps // 2
    blocks = cells // LANES
    assert blocks * rows == LANES and rows % WIN == 0 and half == SUBS and taps == WIN + 1
    sizes = (freqs, rows, cells, level_count, taps, strips)
    table = (level_count * 2 * WIN, 6 * 2 * WIN)
    coeffs = jnp.transpose(coeffs, (0, 2, 1, 3))
    vmem, hbm = [pl.BlockSpec(memory_space=space) for space in (pltpu.VMEM, pltpu.HBM)]
    f32, bf16 = jnp.float32, jnp.bfloat16
    image_shape = (STEPS, rows, cells)
    span = rows + 2 * half
    shape, levels_shape, coeffs_shape, angles_shape = waves.shape, levels.shape, coeffs.shape, angles.shape
    waves, levels, coeffs, angles, order = [
        pltpu.with_memory_space_constraint(v, pltpu.HBM) for v in (waves, levels, coeffs, angles, order)
    ]
    out, image = pl.pallas_call(
        functools.partial(kernel, sizes),
        out_shape=(jax.ShapeDtypeStruct(shape, f32), jax.ShapeDtypeStruct(image_shape, f32)),
        in_specs=[hbm] * 5,
        out_specs=(vmem, vmem),
        scratch_shapes=[
            pltpu.SMEM(order.shape, jnp.int32),
            pltpu.VMEM(levels_shape, jnp.int32),
            pltpu.VMEM(coeffs_shape, f32),
            pltpu.VMEM(angles_shape, f32),
            pltpu.SemaphoreType.DMA((4 + freqs,)),
            pltpu.VMEM((LANES, LANES), jnp.int32),
            pltpu.VMEM((2, level_count, coeffs_shape[2], LANES), f32),
            pltpu.VMEM((2, angles_shape[0], LANES), f32),
            pltpu.VMEM((freqs,) + table, bf16),
            pltpu.VMEM((freqs, rows, cells), f32),
            pltpu.VMEM((freqs, rows, cells), f32),
            pltpu.VMEM((freqs, 2, 2, rows, cells), f32),
            pltpu.VMEM((2, 2, LANES + 2 * half, 2 * LANES), bf16),
            pltpu.VMEM((2, LANES, 2 * LANES), f32),
            pltpu.VMEM((STEPS, freqs, 2, 2, span, cells), f32),
            pltpu.VMEM((2, 2, 2, span, cells), bf16),
            pltpu.SemaphoreType.DMA((STEPS, freqs, 2)),
            pltpu.SemaphoreType.DMA((STEPS, freqs, 2)),
        ],
        compiler_params=pltpu.CompilerParams(
            collective_id=0, has_side_effects=True, vmem_limit_bytes=32 * 1024 * 1024
        ),
    )(waves, levels, coeffs, angles, order)
    return pl.pallas_call(
        store_kernel,
        out_shape=(jax.ShapeDtypeStruct(shape, f32), jax.ShapeDtypeStruct(image_shape, f32)),
        in_specs=[vmem, vmem],
        out_specs=(hbm, hbm),
        scratch_shapes=[pltpu.SemaphoreType.DMA((2,))],
        compiler_params=pltpu.CompilerParams(vmem_limit_bytes=8 * 1024 * 1024),
    )(out, image)


def solution(mesh):
    in_specs = (P(None, None, "shot", "strip", None), P("strip", None), P(), P(), P("shot"))
    out_specs = (P(None, None, "shot", "strip", None), P("shot", "strip", None))
    return jax.shard_map(
        functools.partial(on_device, mesh.shape["strip"]),
        mesh=mesh,
        in_specs=in_specs,
        out_specs=out_specs,
        check_vma=False,
    )
```

time: 30.4 us -> 18 us (0.59)
  Pallas kernels: 25.2 us -> 17.2 us
  local copies, waits for them, and re-layouts: 4.33 us -> 0 us
    pallas_call x1, Pallas kernels: 25.2 us -> 16.2 us  [on_device(): pl.pallas_call(functools.partial(kernel, sizes), out_shape=(jax.ShapeDtyp...]
    unnamed x5 -> x0, local copies, waits for them, and re-layouts: 4.33 us -> none
    pallas_call x0 -> x1, Pallas kernels: none -> 1.02 us  [on_device(): pl.pallas_call(store_kernel, out_shape=(jax.ShapeDtypeStruct(shape, f32),...]
where the time goes in v1:
time: 18 us; the launch traced here: 17.8 us
  Pallas kernels  17.2 us (96%)
  between operations  0.64 us (4%)
    pallas_call x1, Pallas kernels, on_device(): pl.pallas_call(functools.partial(kernel, sizes), out_shape=(jax.ShapeDtyp...  16.2 us
    pallas_call x1, Pallas kernels, on_device(): pl.pallas_call(store_kernel, out_shape=(jax.ShapeDtypeStruct(shape, f32),...  1.02 us

profile of v1, /device:TPU:12, one launch (start us, length us, event | category | flops | bytes accessed | tf_op | source)
XLA Modules:
  0.0 17.8 jit_solution(6356866335195309280)
XLA Ops:
  0.6 16.2 %shard_map.68 = (f32[2,2,4,32,512]{4,3,2,1,0:T(8,128)S(1)}, f32[2,32,512]{2,1,0:T(8,128)S(1)}) custom-call(f32[2,2,4,32,512]{4,3,2,1,0:T(8,128)} %waves_hbm.1, s32[32,512]{1,0:T(8,128)} %levels_hbm.1, f32[2,5,4,17]{3,2,1,0:T(4,128)} %bitcast.1, f32[4,5]{1,0:T(4,128)} %angles_hbm.1, s32[4]{0:T(128)} %order_hbm.1), custom_call_target="tpu_custom_call" | custom-call | tf_op jit(solution)/shard_map/pallas_call | solution.py:283
  16.8 1.0 %shard_map.69 = (f32[2,2,4,32,512]{4,3,2,1,0:T(8,128)}, f32[2,32,512]{2,1,0:T(8,128)}) custom-call(f32[2,2,4,32,512]{4,3,2,1,0:T(8,128)S(1)} %get-tuple-element.4.waves_ref, f32[2,32,512]{2,1,0:T(8,128)S(1)} %get-tuple-element.5.image_ref), custom_call_target="tpu_custom_call" | custom-call | tf_op jit(solution)/shard_map/pallas_call | solution.py:312

commit v2 on v1

--- a/solution.py
+++ b/solution.py
@@ -11,6 +11,7 @@
 LANES = 128
 SUBS = 8
 WIN = 16
+RAW = 1
 MESH = pl.DeviceIdType.MESH
 
 
@@ -44,6 +45,7 @@
     order_ref, level_ref, coef_ref, angle_ref, load_sem,
     turned_ref, base_ref, turn_ref, table_ref, cos_ref, sin_ref,
     field_ref, part_ref, pass_ref, mid_ref, cross_ref, send_sem, recv_sem,
+    edge_level_ref, edge_turned_ref, edge_ref, edge_part_ref, edge_pass_ref, raw_send_sem, raw_recv_sem,
 ):
     freqs, rows, cells, levels, taps, strips = sizes
     half = taps // 2
@@ -51,30 +53,66 @@
     me = lax.axis_index("strip")
     has_low, has_high = me > 0, me < strips - 1
 
+    def neighbour(step):
+        return {"strip": me + step}
+
+    barrier = pltpu.get_barrier_semaphore()
+    for there, step in ((has_low, -1), (has_high, 1)):
+
+        @pl.when(there)
+        def _():
+            pl.semaphore_signal(barrier, inc=1, device_id=neighbour(step), device_id_type=MESH)
+
     small = [
         pltpu.make_async_copy(source, target, load_sem.at[i])
         for i, (source, target) in enumerate(
             ((coeffs_hbm, coef_ref), (angles_hbm, angle_ref), (levels_hbm, level_ref), (order_hbm, order_ref))
         )
     ]
+    def wave_load(f):
+        return pltpu.make_async_copy(waves_hbm.at[:, :, f], field_ref.at[f], load_sem.at[4 + f])
+
+    early = lax.rem(me, 2) == 0
+    skip = jnp.where(early, RAW, 0)
+
+    def turn_of(i):
+        return lax.rem(i + skip, freqs)
+
+    def raw_copy(f):
+        if f is None:
+            source, target, at = levels_hbm.at[pl.ds(0, half), :], edge_level_ref, 0
+        else:
+            source, target, at = waves_hbm.at[:, :, f, pl.ds(0, half), :], edge_ref.at[f], f + 1
+        return pltpu.make_async_remote_copy(
+            src_ref=source,
+            dst_ref=target,
+            send_sem=raw_send_sem.at[at],
+            recv_sem=raw_recv_sem.at[at],
+            device_id=neighbour(-1),
+            device_id_type=MESH,
+        )
+
+    def enter():
+        pl.semaphore_wait(barrier, has_low.astype(jnp.int32) + has_high.astype(jnp.int32))
+
+    sends_raw = jnp.logical_and(early, has_low)
+    gets_raw = jnp.logical_and(jnp.logical_not(early), has_high)
+
+    @pl.when(early)
+    def _():
+        enter()
+
+    @pl.when(sends_raw)
+    def _():
+        for f in [*range(RAW), None]:
+            raw_copy(f).start()
+
+    wave_load(turn_of(0)).start()
     for load in small:
         load.start()
 
-    def wave_load(f):
-        return pltpu.make_async_copy(waves_hbm.at[:, :, f], field_ref.at[f], load_sem.at[4 + f])
-
-    for f in range(freqs):
-        wave_load(f).start()
-
-    def neighbour(step):
-        return {"strip": me + step}
-
-    barrier = pltpu.get_barrier_semaphore()
-    for there, step in ((has_low, -1), (has_high, 1)):
-
-        @pl.when(there)
-        def _():
-            pl.semaphore_signal(barrier, inc=1, device_id=neighbour(step), device_id_type=MESH)
+    for i in range(1, freqs):
+        wave_load(turn_of(i)).start()
 
     lane = lax.broadcasted_iota(jnp.int32, (SUBS, LANES), 1)
 
@@ -114,6 +152,48 @@
     stacked = jnp.concatenate([level_ref[:, q * LANES : (q + 1) * LANES] for q in range(blocks)], axis=0)
     turned_ref[...] = stacked.T
 
+    def stack(v):
+        return jnp.concatenate([v[:, q * LANES : (q + 1) * LANES] for q in range(blocks)], axis=0)
+
+    def margins(v, count, width):
+        place = lax.rem(lane, width)
+        before = jnp.where(place >= count, pltpu.roll(v[LANES - half :], count, 1), 0.0)
+        after = jnp.where(place < width - count, pltpu.roll(v[:half], LANES - count, 1), 0.0)
+        return jnp.concatenate([before, v, after], axis=0)
+
+    def turn_entries(which, f):
+        line = turn_ref[which, pl.ds(order_ref[f], 1), :]
+        return [jnp.broadcast_to(line[:, i : i + 1], (SUBS, LANES)) for i in range(levels)]
+
+    def edge_pass(f):
+        level = stack(edge_level_ref[...])
+        cosine, sine = [
+            pick(level, [jnp.concatenate([e] * blocks, axis=0) for e in turn_entries(which, f)]) for which in range(2)
+        ]
+        reals, imags = [], []
+        for field in range(2):
+            real, imag = [stack(edge_ref[f, field, comp]) for comp in range(2)]
+            if field == 1:
+                imag = -imag
+            reals.append(real * cosine - imag * sine)
+            imags.append(real * sine + imag * cosine)
+        v = margins(jnp.concatenate(reals + imags, axis=0).T, half, LANES // 4)
+        for comp, u in enumerate((v, pltpu.roll(v, LANES // 2, 1))):
+            for part, piece in enumerate(split(u)):
+                edge_part_ref[part, comp] = piece
+        table = table_ref[f]
+        low_lanes = lax.broadcasted_iota(jnp.int32, (WIN, LANES), 1) < LANES // 2
+        for b in range(0, LANES, WIN):
+            parts = [[edge_part_ref[part, comp, b : b + 2 * WIN, :] for comp in range(2)] for part in range(2)]
+            real, imag = filtered(table, parts, edge_turned_ref[b : b + WIN, :])
+            edge_pass_ref[b : b + WIN, :] = jnp.where(low_lanes, real, pltpu.roll(imag, LANES // 2, 1))
+        v = edge_pass_ref[...].T
+        for comp in range(2):
+            for field in range(2):
+                for q in range(blocks):
+                    at = ((comp * 2 + field) * blocks + q) * half
+                    mid_ref[0, f, field, comp, half + rows :, q * LANES : (q + 1) * LANES] = v[at : at + half]
+
     def prepare(f):
         row = pl.ds(order_ref[f], 1)
         for level in range(levels):
@@ -124,8 +204,7 @@
                 table_ref[f, at : at + WIN, :LANES] = high
                 table_ref[f, at : at + WIN, LANES:] = low[:, : 4 * WIN]
         for which, target in enumerate((cos_ref, sin_ref)):
-            line = turn_ref[which, row, :]
-            entries = [jnp.broadcast_to(line[:, i : i + 1], (SUBS, LANES)) for i in range(levels)]
+            entries = turn_entries(which, f)
             for top in range(0, rows, SUBS):
                 for q in range(blocks):
                     level = level_ref[top : top + SUBS, q * LANES : (q + 1) * LANES]
@@ -200,34 +279,55 @@
             device_id_type=MESH,
         )
 
+    def outgoing(step, f):
+        if step == 0:
+            return jnp.logical_and(has_low, jnp.logical_or(jnp.logical_not(early), f >= RAW)), has_high
+        return has_low, has_high
+
+    def incoming(step, f):
+        if step == 0:
+            return has_low, jnp.logical_and(has_high, jnp.logical_or(early, f >= RAW))
+        return has_low, has_high
+
     def send(step, f):
-        for side, there in enumerate((has_low, has_high)):
+        for side, there in enumerate(outgoing(step, f)):
 
             @pl.when(there)
             def _():
                 halo_copy(step, f, side).start()
 
     def receive(step, f):
-        for side, there in ((1, has_low), (0, has_high)):
+        for side, there in enumerate(incoming(step, f)):
 
             @pl.when(there)
             def _():
-                halo_copy(step, f, side).wait_recv()
+                halo_copy(step, f, 1 - side).wait_recv()
 
     image_ref[...] = jnp.zeros_like(image_ref)
 
-    prepare(0)
-    wave_load(0).wait()
-    inline_pass(0, 0)
-    pl.semaphore_wait(barrier, has_low.astype(jnp.int32) + has_high.astype(jnp.int32))
-    send(0, 0)
-
-    @pl.loop(1, freqs)
-    def _(f):
+    @pl.loop(0, freqs)
+    def _(i):
+        f = turn_of(i)
         prepare(f)
         wave_load(f).wait()
         inline_pass(0, f)
+
+        @pl.when(jnp.logical_and(i == 0, jnp.logical_not(early)))
+        def _():
+            enter()
+
         send(0, f)
+
+    @pl.when(gets_raw)
+    def _():
+        raw_copy(None).wait_recv()
+        edge = stack(edge_level_ref[...])
+        edge_turned_ref[...] = jnp.concatenate([edge] * 4, axis=0).T
+
+        @pl.loop(0, RAW)
+        def _(f):
+            raw_copy(f).wait_recv()
+            edge_pass(f)
 
     @pl.loop(0, freqs)
     def _(f):
@@ -241,11 +341,16 @@
         receive(1, f)
         cross_pass(1, f)
 
+    @pl.when(sends_raw)
+    def _():
+        for f in [*range(RAW), None]:
+            raw_copy(f).wait_send()
+
     for step in range(STEPS):
 
         @pl.loop(0, freqs)
         def _(f):
-            for side, there in enumerate((has_low, has_high)):
+            for side, there in enumerate(outgoing(step, f)):
 
                 @pl.when(there)
                 def _():
@@ -304,6 +409,13 @@
             pltpu.VMEM((2, 2, 2, span, cells), bf16),
             pltpu.SemaphoreType.DMA((STEPS, freqs, 2)),
             pltpu.SemaphoreType.DMA((STEPS, freqs, 2)),
+            pltpu.VMEM((half, cells), jnp.int32),
+            pltpu.VMEM((LANES, LANES), jnp.int32),
+            pltpu.VMEM((RAW, 2, 2, half, cells), f32),
+            pltpu.VMEM((2, 2, LANES + 2 * half, LANES), bf16),
+            pltpu.VMEM((LANES, LANES), f32),
+            pltpu.SemaphoreType.DMA((RAW + 1,)),
+            pltpu.SemaphoreType.DMA((RAW + 1,)),
         ],
         compiler_params=pltpu.CompilerParams(
             collective_id=0, has_side_effects=True, vmem_limit_bytes=32 * 1024 * 1024

time: 18 us -> 17.4 us (0.967)
  Pallas kernels: 17.2 us -> 16.6 us
    pallas_call x1, Pallas kernels: 16.2 us -> 15.6 us  [on_device(): pl.pallas_call(functools.partial(kernel, sizes), out_shape=(jax.ShapeDtyp...]
where the time goes in v2:
time: 17.4 us; the launch traced here: 17.3 us
  Pallas kernels  16.6 us (95%)
  between operations  0.64 us (4%)
    pallas_call x1, Pallas kernels, on_device(): pl.pallas_call(functools.partial(kernel, sizes), out_shape=(jax.ShapeDtyp...  15.6 us
    pallas_call x1, Pallas kernels, on_device(): pl.pallas_call(store_kernel, out_shape=(jax.ShapeDtypeStruct(shape, f32),...  1.02 us

profile of v2, /device:TPU:12, one launch (start us, length us, event | category | flops | bytes accessed | tf_op | source)
XLA Modules:
  0.0 17.3 jit_solution(14026035058342368360)
XLA Ops:
  0.6 15.6 %shard_map.68 = (f32[2,2,4,32,512]{4,3,2,1,0:T(8,128)S(1)}, f32[2,32,512]{2,1,0:T(8,128)S(1)}) custom-call(f32[2,2,4,32,512]{4,3,2,1,0:T(8,128)} %waves_hbm.1, s32[32,512]{1,0:T(8,128)} %levels_hbm.1, f32[2,5,4,17]{3,2,1,0:T(4,128)} %bitcast.1, f32[4,5]{1,0:T(4,128)} %angles_hbm.1, s32[4]{0:T(128)} %order_hbm.1), custom_call_target="tpu_custom_call" | custom-call | tf_op jit(solution)/shard_map/pallas_call | solution.py:388
  16.2 1.0 %shard_map.69 = (f32[2,2,4,32,512]{4,3,2,1,0:T(8,128)}, f32[2,32,512]{2,1,0:T(8,128)}) custom-call(f32[2,2,4,32,512]{4,3,2,1,0:T(8,128)S(1)} %get-tuple-element.4.waves_ref, f32[2,32,512]{2,1,0:T(8,128)S(1)} %get-tuple-element.5.image_ref), custom_call_target="tpu_custom_call" | custom-call | tf_op jit(solution)/shard_map/pallas_call | solution.py:424

commit v3 on v2

--- a/solution.py
+++ b/solution.py
@@ -40,11 +40,32 @@
     ]
 
 
+def cross_window(table, level_ref, cross_ref, first, store):
+    wide = 2 * LANES
+    for x in range(0, level_ref.shape[1], wide):
+        at = (pl.ds(first, WIN), slice(x, x + wide))
+        level = level_ref[at]
+        sums = []
+        for field in range(2):
+            parts = [
+                [cross_ref[part, field, comp, pl.ds(first, 2 * WIN), x : x + wide] for comp in range(2)]
+                for part in range(2)
+            ]
+            sums.append(filtered(table, parts, level))
+        store(at, sums)
+
+
+def windows(me, rows):
+    late = lax.rem(me, 2) * (rows - WIN)
+    return [pl.multiple_of(first, WIN) for first in (rows - WIN - late, late)]
+
+
 def kernel(
-    sizes, waves_hbm, levels_hbm, coeffs_hbm, angles_hbm, order_hbm, out_ref, image_ref,
-    order_ref, level_ref, coef_ref, angle_ref, load_sem,
-    turned_ref, base_ref, turn_ref, table_ref, cos_ref, sin_ref,
-    field_ref, part_ref, pass_ref, mid_ref, cross_ref, send_sem, recv_sem,
+    sizes, waves_hbm, levels_hbm, coeffs_hbm, angles_hbm, order_hbm,
+    out_ref, image_ref, table_ref, level_ref, cross_ref,
+    order_ref, coef_ref, angle_ref, load_sem,
+    turned_ref, base_ref, turn_ref, cos_ref, sin_ref,
+    field_ref, part_ref, pass_ref, mid_ref, send_sem, recv_sem,
     edge_level_ref, edge_turned_ref, edge_ref, edge_part_ref, edge_pass_ref, raw_send_sem, raw_recv_sem,
 ):
     freqs, rows, cells, levels, taps, strips = sizes
@@ -239,34 +260,30 @@
                         q * rows : (q + 1) * rows
                     ]
 
-    def cross_pass(step, f):
-        last = step == STEPS - 1
+    def split_rows(step, f, first, count):
         for field in range(2):
             for comp in range(2):
-                for part, piece in enumerate(split(mid_ref[step, f, field, comp])):
-                    cross_ref[part, field, comp] = piece
-        table = table_ref[f]
-        wide = 2 * LANES
-        for b in range(0, rows, WIN):
-            for x in range(0, cells, wide):
-                at = (slice(b, b + WIN), slice(x, x + wide))
-                level = level_ref[at]
-                sums = []
-                for field in range(2):
-                    parts = [
-                        [cross_ref[part, field, comp, b : b + 2 * WIN, x : x + wide] for comp in range(2)]
-                        for part in range(2)
-                    ]
-                    sums.append(filtered(table, parts, level))
-                (sr, si), (qr, qi) = sums
-                for field in range(2):
-                    for comp in range(2):
-                        v = sums[field][comp]
-                        if last:
-                            out_ref[(field, comp, f) + at] = -v if field and comp else v
-                        else:
-                            field_ref[(f, field, comp) + at] = v
-                image_ref[(step,) + at] += sr * qr - si * qi
+                for part, piece in enumerate(split(mid_ref[step, f, field, comp, pl.ds(first, count), :])):
+                    cross_ref[part, field, comp, pl.ds(first, count), :] = piece
+
+    def cross_rows(step, f, first):
+        def store(at, sums):
+            (sr, si), (qr, qi) = sums
+            for field in range(2):
+                for comp in range(2):
+                    v = sums[field][comp]
+                    if step == STEPS - 1:
+                        out_ref[(field, comp, f) + at] = -v if field and comp else v
+                    else:
+                        field_ref[(f, field, comp) + at] = v
+            image_ref[(step,) + at] += sr * qr - si * qi
+
+        cross_window(table_ref[f], level_ref, cross_ref, first, store)
+
+    def cross_pass(step, f):
+        split_rows(step, f, 0, rows + 2 * half)
+        for first in range(0, rows, WIN):
+            cross_rows(step, f, first)
 
     def halo_copy(step, f, side):
         source, target = ((half, rows + half), (rows, 0))[side]
@@ -296,8 +313,10 @@
             def _():
                 halo_copy(step, f, side).start()
 
-    def receive(step, f):
+    def receive(step, f, which=None):
         for side, there in enumerate(incoming(step, f)):
+            if which is not None:
+                there = jnp.logical_and(there, which[side])
 
             @pl.when(there)
             def _():
@@ -336,10 +355,17 @@
         inline_pass(1, f)
         send(1, f)
 
-    @pl.loop(0, freqs)
+    @pl.loop(0, freqs - 1)
     def _(f):
         receive(1, f)
         cross_pass(1, f)
+
+    soon, late = windows(me, rows)
+    receive(1, freqs - 1, (jnp.logical_not(early), early))
+    split_rows(1, freqs - 1, soon, 2 * WIN)
+    cross_rows(1, freqs - 1, soon)
+    receive(1, freqs - 1, (early, jnp.logical_not(early)))
+    split_rows(1, freqs - 1, late, 2 * WIN)
 
     @pl.when(sends_raw)
     def _():
@@ -357,12 +383,37 @@
                     halo_copy(step, f, side).wait_send()
 
 
-def store_kernel(waves_ref, image_ref, waves_hbm, image_hbm, sem):
+def store_kernel(waves_ref, image_ref, table_ref, level_ref, cross_ref, waves_hbm, image_hbm, last_ref, sum_ref, sem):
+    freqs, rows = waves_ref.shape[2:4]
+    soon, late = windows(lax.axis_index("strip"), rows)
+    done, step = freqs - 1, image_ref.shape[0] - 1
+    early, after = pl.ds(soon, WIN), pl.ds(late, WIN)
     copies = [
-        pltpu.make_async_copy(waves_ref, waves_hbm, sem.at[0]),
-        pltpu.make_async_copy(image_ref, image_hbm, sem.at[1]),
+        pltpu.make_async_copy(source, target, sem.at[i])
+        for i, (source, target) in enumerate(
+            (
+                (waves_ref.at[:, :, pl.ds(0, done)], waves_hbm.at[:, :, pl.ds(0, done)]),
+                (image_ref.at[pl.ds(0, step)], image_hbm.at[pl.ds(0, step)]),
+                (waves_ref.at[:, :, done, early], waves_hbm.at[:, :, done, early]),
+                (image_ref.at[step, early], image_hbm.at[step, early]),
+                (last_ref, waves_hbm.at[:, :, done, after]),
+                (sum_ref, image_hbm.at[step, after]),
+            )
+        )
     ]
-    for copy in copies:
+    for copy in copies[:4]:
+        copy.start()
+
+    def store(at, sums):
+        (sr, si), (qr, qi) = sums
+        for field in range(2):
+            for comp in range(2):
+                v = sums[field][comp]
+                last_ref[field, comp, :, at[1]] = -v if field and comp else v
+        sum_ref[:, at[1]] = image_ref[(step,) + at] + sr * qr - si * qi
+
+    cross_window(table_ref[done], level_ref, cross_ref, late, store)
+    for copy in copies[4:]:
         copy.start()
     for copy in copies:
         copy.wait()
@@ -373,7 +424,7 @@
     level_count, taps = coeffs.shape[2:]
     half = taps // 2
     blocks = cells // LANES
-    assert blocks * rows == LANES and rows % WIN == 0 and half == SUBS and taps == WIN + 1
+    assert blocks * rows == LANES and rows == 2 * WIN and half == SUBS and taps == WIN + 1
     sizes = (freqs, rows, cells, level_count, taps, strips)
     table = (level_count * 2 * WIN, 6 * 2 * WIN)
     coeffs = jnp.transpose(coeffs, (0, 2, 1, 3))
@@ -385,28 +436,32 @@
     waves, levels, coeffs, angles, order = [
         pltpu.with_memory_space_constraint(v, pltpu.HBM) for v in (waves, levels, coeffs, angles, order)
     ]
-    out, image = pl.pallas_call(
+    held = (
+        jax.ShapeDtypeStruct(shape, f32),
+        jax.ShapeDtypeStruct(image_shape, f32),
+        jax.ShapeDtypeStruct((freqs,) + table, bf16),
+        jax.ShapeDtypeStruct(levels_shape, jnp.int32),
+        jax.ShapeDtypeStruct((2, 2, 2, span, cells), bf16),
+    )
+    held = pl.pallas_call(
         functools.partial(kernel, sizes),
-        out_shape=(jax.ShapeDtypeStruct(shape, f32), jax.ShapeDtypeStruct(image_shape, f32)),
+        out_shape=held,
         in_specs=[hbm] * 5,
-        out_specs=(vmem, vmem),
+        out_specs=(vmem,) * len(held),
         scratch_shapes=[
             pltpu.SMEM(order.shape, jnp.int32),
-            pltpu.VMEM(levels_shape, jnp.int32),
             pltpu.VMEM(coeffs_shape, f32),
             pltpu.VMEM(angles_shape, f32),
             pltpu.SemaphoreType.DMA((4 + freqs,)),
             pltpu.VMEM((LANES, LANES), jnp.int32),
             pltpu.VMEM((2, level_count, coeffs_shape[2], LANES), f32),
             pltpu.VMEM((2, angles_shape[0], LANES), f32),
-            pltpu.VMEM((freqs,) + table, bf16),
             pltpu.VMEM((freqs, rows, cells), f32),
             pltpu.VMEM((freqs, rows, cells), f32),
             pltpu.VMEM((freqs, 2, 2, rows, cells), f32),
             pltpu.VMEM((2, 2, LANES + 2 * half, 2 * LANES), bf16),
             pltpu.VMEM((2, LANES, 2 * LANES), f32),
             pltpu.VMEM((STEPS, freqs, 2, 2, span, cells), f32),
-            pltpu.VMEM((2, 2, 2, span, cells), bf16),
             pltpu.SemaphoreType.DMA((STEPS, freqs, 2)),
             pltpu.SemaphoreType.DMA((STEPS, freqs, 2)),
             pltpu.VMEM((half, cells), jnp.int32),
@@ -424,11 +479,15 @@
     return pl.pallas_call(
         store_kernel,
         out_shape=(jax.ShapeDtypeStruct(shape, f32), jax.ShapeDtypeStruct(image_shape, f32)),
-        in_specs=[vmem, vmem],
+        in_specs=[vmem] * len(held),
         out_specs=(hbm, hbm),
-        scratch_shapes=[pltpu.SemaphoreType.DMA((2,))],
+        scratch_shapes=[
+            pltpu.VMEM((2, 2, WIN, cells), f32),
+            pltpu.VMEM((WIN, cells), f32),
+            pltpu.SemaphoreType.DMA((6,)),
+        ],
         compiler_params=pltpu.CompilerParams(vmem_limit_bytes=8 * 1024 * 1024),
-    )(out, image)
+    )(*held)
 
 
 def solution(mesh):

time: 17.4 us -> 17.1 us (0.983)
  Pallas kernels: 16.6 us -> 16.3 us
    pallas_call x1, Pallas kernels: 15.6 us -> 15.3 us  [on_device(): pl.pallas_call(functools.partial(kernel, sizes), out_shape=held, in_specs...]
where the time goes in v3:
time: 17.1 us; the launch traced here: 17 us
  Pallas kernels  16.3 us (95%)
  between operations  0.64 us (4%)
    pallas_call x1, Pallas kernels, on_device(): pl.pallas_call(functools.partial(kernel, sizes), out_shape=held, in_specs...  15.3 us
    pallas_call x1, Pallas kernels, on_device(): pl.pallas_call(store_kernel, out_shape=(jax.ShapeDtypeStruct(shape, f32),...  1.08 us

profile of v3, /device:TPU:12, one launch (start us, length us, event | category | flops | bytes accessed | tf_op | source)
XLA Modules:
  0.0 17.0 jit_solution(14082415429304079964)
XLA Ops:
  0.6 15.3 %shard_map.68 = (f32[2,2,4,32,512]{4,3,2,1,0:T(8,128)S(1)}, f32[2,32,512]{2,1,0:T(8,128)S(1)}, bf16[4,160,192]{2,1,0:T(8,128)(2,1)S(1)}, s32[32,512]{1,0:T(8,128)S(1)}, bf16[2,2,2,48,512]{4,3,2,1,0:T(8,128)(2,1)S(1)}) custom-call(f32[2,2,4,32,512]{4,3,2,1,0:T(8,128)} %waves_hbm.1, s32[32,512]{1,0:T(8,128)} %levels_hbm.1, f32[2,5,4,17]{3,2,1,0:T(4,128)} %bitcast.1, ...), custom_call_target="tpu_custom_call" | custom-call | tf_op jit(solution)/shard_map/pallas_call | solution.py:446
  15.9 1.1 %shard_map.69 = (f32[2,2,4,32,512]{4,3,2,1,0:T(8,128)}, f32[2,32,512]{2,1,0:T(8,128)}) custom-call(f32[2,2,4,32,512]{4,3,2,1,0:T(8,128)S(1)} %get-tuple-element.7.waves_ref, f32[2,32,512]{2,1,0:T(8,128)S(1)} %get-tuple-element.8.image_ref, bf16[4,160,192]{2,1,0:T(8,128)(2,1)S(1)} %get-tuple-element.9.table_ref, s32[32,512]{1,0:T(8,128)S(1)} %get-tuple-element.10.level_ref, ...), custom_call_target="tpu_custom_call" | custom-call | tf_op jit(solution)/shard_map/pallas_call | solution.py:479
